TPU v7x, 256 devices: a whole 4x4x8 slice. The times are simulated.
256 devices in a mesh: gx: 8 (over y, core), gy: 32 (over x, z).
Axes of the slice: x: 4, y: 4, z: 8, core: 2. Of those that a mesh axis runs over, the one named last changes fastest.
Arguments:
- flow_field: float32 [16, 256, 256, 128], P(None, 'gx', 'gy'), may hold values from -6 to 6
- cotangent: float32 [16, 256, 256, 128], P(None, 'gx', 'gy'), may hold values from -6 to 6
- mode_weights: float32 [4, 16, 16, 256], replicated, may hold values from -3 to 3
- point_weights: float32 [16, 16], replicated, may hold values from -1.5 to 1.5
- point_bias: float32 [16], replicated, may hold values from -3 to 3
Outputs:
- output_field: float32 [16, 256, 256, 128], P(None, 'gx', 'gy')
- grad_field: float32 [16, 256, 256, 128], P(None, 'gx', 'gy')
- grad_modes: float32 [4, 16, 16, 256], replicated
- grad_point: float32 [16, 16], replicated
- grad_bias: float32 [16], replicated
All inputs are finite; a program needn't handle non-finite values.
Results may differ from a plain program's by a relative error of at most 0.00024.
Values sent between devices are 32-bit elements; how exact they have to be, the bound alone decides.
No kernel may reach another device: no remote copies, remote signals or barrier semaphores. Data moves between devices by JAX's collectives and lax.ppermute only.
A program may use at most 128 MiB of HBM per device.

v0:
```python
import math
import jax
import jax.numpy as jnp
from jax import lax
from jax.sharding import PartitionSpec as P

LOW_PASS = [
    0.23037781330885523,
    0.7148465705525415,
    0.6308807679295904,
    -0.02798376941698385,
    -0.18703481171888114,
    0.030841381835986965,
    0.032883011666982945,
    -0.010597401784997278,
]
HIGH_PASS = [(-1) ** position * LOW_PASS[7 - position] for position in range(8)]
GELU_SCALE = 0.7978845608028654
GELU_CUBE = 0.044715


def from_behind(value, axis, by):
    devices = lax.axis_size(axis)
    return lax.ppermute(value, axis, [(i, (i + by) % devices) for i in range(devices)])


def filter_table(filter_taps, out_count, in_count, periodic):
    row_index = lax.broadcasted_iota(jnp.int32, (out_count, in_count), 0)
    col_index = lax.broadcasted_iota(jnp.int32, (out_count, in_count), 1)
    offset = col_index - 2 * row_index
    if periodic:
        offset = offset % in_count
    matrix = jnp.zeros((out_count, in_count), jnp.float32)
    for position in range(8):
        matrix = matrix + filter_taps[position] * (offset == position).astype(jnp.float32)
    return matrix


def lifted_table(filter_taps, out_count, in_count):
    row_index = lax.broadcasted_iota(jnp.int32, (out_count, in_count), 0)
    col_index = lax.broadcasted_iota(jnp.int32, (out_count, in_count), 1)
    offset = row_index - 2 * col_index + 6
    matrix = jnp.zeros((out_count, in_count), jnp.float32)
    for position in range(8):
        matrix = matrix + filter_taps[position] * (offset == position).astype(jnp.float32)
    return matrix


def along_x(matrix, signal):
    return jnp.einsum("kr,arys->akys", matrix, signal, precision=lax.Precision.HIGHEST)


def along_y(matrix, signal):
    return jnp.einsum("kr,axrs->axks", matrix, signal, precision=lax.Precision.HIGHEST)


def plane_x(matrix, signal):
    return jnp.einsum("kr,ary->aky", matrix, signal, precision=lax.Precision.HIGHEST)


def plane_y(matrix, signal):
    return jnp.einsum("kr,axr->axk", matrix, signal, precision=lax.Precision.HIGHEST)


def to_lanes(signal):
    channels, extent_x, extent_y, planes = signal.shape
    return jnp.transpose(signal, (0, 3, 1, 2)).reshape(channels * planes, extent_x, extent_y)


def from_lanes(signal, channels):
    stacked, extent_x, extent_y = signal.shape
    return jnp.transpose(
        signal.reshape(channels, stacked // channels, extent_x, extent_y), (0, 2, 3, 1)
    )


def four_bands(signal):
    extent_x, extent_y = (signal.shape[1], signal.shape[2])
    low_x = plane_x(filter_table(LOW_PASS, extent_x // 2, extent_x, True), signal)
    high_x = plane_x(filter_table(HIGH_PASS, extent_x // 2, extent_x, True), signal)
    low_y = filter_table(LOW_PASS, extent_y // 2, extent_y, True)
    high_y = filter_table(HIGH_PASS, extent_y // 2, extent_y, True)
    return jnp.stack(
        [
            plane_y(low_y, low_x),
            plane_y(low_y, high_x),
            plane_y(high_y, low_x),
            plane_y(high_y, high_x),
        ]
    )


def join_bands(changes):
    modes_x, modes_y = (changes.shape[2], changes.shape[3])
    low_x = filter_table(LOW_PASS, modes_x, 2 * modes_x, True).T
    high_x = filter_table(HIGH_PASS, modes_x, 2 * modes_x, True).T
    low_y = filter_table(LOW_PASS, modes_y, 2 * modes_y, True).T
    high_y = filter_table(HIGH_PASS, modes_y, 2 * modes_y, True).T
    from_low = plane_y(low_y, changes[0]) + plane_y(high_y, changes[2])
    from_high = plane_y(low_y, changes[1]) + plane_y(high_y, changes[3])
    return plane_x(low_x, from_low) + plane_x(high_x, from_high)


def gelu_parts(signal):
    tangent = jnp.tanh(GELU_SCALE * (signal + GELU_CUBE * signal * signal * signal))
    activated = 0.5 * signal * (1.0 + tangent)
    gelu_slope = 0.5 * (1.0 + tangent) + 0.5 * signal * (1.0 - tangent * tangent) * GELU_SCALE * (
        1.0 + 3.0 * GELU_CUBE * signal * signal
    )
    return (activated, gelu_slope)


def wave_block(signal, weights_grid, transposed):
    x_index = lax.axis_index("gx")
    channels = signal.shape[0]
    extent_x, extent_y = (signal.shape[1], signal.shape[2])
    margin = from_behind(signal[:, :6], "gx", -1)
    halved = along_x(
        filter_table(LOW_PASS, extent_x // 2, extent_x + 6, False),
        jnp.concatenate([signal, margin], 1),
    )
    margin = from_behind(halved[:, :, :6], "gy", -1)
    level_one = along_y(
        filter_table(LOW_PASS, extent_y // 2, extent_y + 6, False),
        jnp.concatenate([halved, margin], 2),
    )
    level_one = to_lanes(lax.all_to_all(level_one, "gy", split_axis=3, concat_axis=2, tiled=True))
    rows_one, cols_one = (level_one.shape[1], level_one.shape[2])
    margin = from_behind(level_one[:, :6], "gx", -1)
    level_two = plane_x(
        filter_table(LOW_PASS, rows_one // 2, rows_one + 6, False),
        jnp.concatenate([level_one, margin], 1),
    )
    level_two = plane_y(filter_table(LOW_PASS, cols_one // 2, cols_one, True), level_two)
    rows_two, cols_two = (level_two.shape[1], level_two.shape[2])
    margin = from_behind(level_two[:, :6], "gx", -1)
    level_three = plane_x(
        filter_table(LOW_PASS, rows_two // 2, rows_two + 6, False),
        jnp.concatenate([level_two, margin], 1),
    )
    level_three = plane_y(filter_table(LOW_PASS, cols_two // 2, cols_two, True), level_three)
    gathered = lax.all_gather(level_three, "gx", axis=1, tiled=True)
    wave_bands = four_bands(gathered)
    stacked, modes_x, modes_y = (wave_bands.shape[1], wave_bands.shape[2], wave_bands.shape[3])
    split_bands = wave_bands.reshape(4, channels, stacked // channels, modes_x, modes_y)
    if transposed:
        mixed_bands = jnp.einsum(
            "bozxy,bioxy->bizxy", split_bands, weights_grid, precision=lax.Precision.HIGHEST
        )
    else:
        mixed_bands = jnp.einsum(
            "bizxy,bioxy->bozxy", split_bands, weights_grid, precision=lax.Precision.HIGHEST
        )
    delta_three = join_bands((mixed_bands - split_bands).reshape(4, stacked, modes_x, modes_y))
    own_rows = rows_two // 2
    own_part = lax.dynamic_slice_in_dim(delta_three, x_index * own_rows, own_rows, 1)
    margin = from_behind(own_part[:, own_rows - 3 :], "gx", 1)
    delta_two = plane_x(
        lifted_table(LOW_PASS, 2 * own_rows, own_rows + 3), jnp.concatenate([margin, own_part], 1)
    )
    cols_three = own_part.shape[2]
    delta_two = plane_y(filter_table(LOW_PASS, cols_three, 2 * cols_three, True).T, delta_two)
    margin = from_behind(delta_two[:, rows_two - 3 :], "gx", 1)
    delta_one = plane_x(
        lifted_table(LOW_PASS, 2 * rows_two, rows_two + 3), jnp.concatenate([margin, delta_two], 1)
    )
    delta_one = plane_y(filter_table(LOW_PASS, cols_two, 2 * cols_two, True).T, delta_one)
    returned = lax.all_to_all(
        from_lanes(delta_one, channels), "gy", split_axis=2, concat_axis=3, tiled=True
    )
    rows_back = returned.shape[1]
    margin = from_behind(returned[:, rows_back - 3 :], "gx", 1)
    widened = along_x(
        lifted_table(LOW_PASS, 2 * rows_back, rows_back + 3), jnp.concatenate([margin, returned], 1)
    )
    cols_back = widened.shape[2]
    margin = from_behind(widened[:, :, cols_back - 3 :], "gy", 1)
    delta_zero = along_y(
        lifted_table(LOW_PASS, 2 * cols_back, cols_back + 3), jnp.concatenate([margin, widened], 2)
    )
    return (signal + delta_zero, split_bands)


def local(flow_field, cotangent, mode_weights, point_weights, point_bias):
    channels = flow_field.shape[0]
    modes_x = flow_field.shape[1] * lax.axis_size("gx") // 16
    modes_y = flow_field.shape[2] * lax.axis_size("gy") // 16
    weights_grid = mode_weights.reshape(4, channels, channels, modes_x, modes_y)
    spectral_flow, bands_flow = wave_block(flow_field, weights_grid, False)
    pointwise = jnp.einsum(
        "io,ixys->oxys", point_weights, flow_field, precision=lax.Precision.HIGHEST
    )
    before_gelu = spectral_flow + pointwise + point_bias[:, None, None, None]
    output_field, gelu_slope = gelu_parts(before_gelu)
    grad_inner = cotangent * gelu_slope
    spectral_grad, bands_grad = wave_block(grad_inner, weights_grid, True)
    point_back = jnp.einsum(
        "io,oxys->ixys", point_weights, grad_inner, precision=lax.Precision.HIGHEST
    )
    grad_field = spectral_grad + point_back
    mode_local = jnp.einsum(
        "bizxy,bozxy->bioxy", bands_flow, bands_grad, precision=lax.Precision.HIGHEST
    )
    mode_local = mode_local.reshape(4, channels, channels, modes_x * modes_y)
    mode_total = lax.psum(mode_local, "gy")
    point_local = jnp.einsum(
        "ixys,oxys->io", flow_field, grad_inner, precision=lax.Precision.HIGHEST
    )
    bias_local = jnp.sum(grad_inner, axis=(1, 2, 3))
    point_total, bias_total = lax.psum((point_local, bias_local), ("gx", "gy"))
    plane_total = flow_field.shape[3]
    cell_count = (
        plane_total
        * flow_field.shape[1]
        * flow_field.shape[2]
        * lax.axis_size("gx")
        * lax.axis_size("gy")
    )
    grad_modes = mode_total / math.sqrt(plane_total)
    grad_point = point_total / math.sqrt(cell_count)
    grad_bias = bias_total / math.sqrt(cell_count)
    return (output_field, grad_field, grad_modes, grad_point, grad_bias)


def solution(mesh):
    in_specs = (P(None, "gx", "gy", None), P(None, "gx", "gy", None), P(), P(), P())
    out_specs = (P(None, "gx", "gy", None), P(None, "gx", "gy", None), P(), P(), P())
    return jax.shard_map(local, mesh=mesh, in_specs=in_specs, out_specs=out_specs, check_vma=False)
```

profile of v0, /device:TPU:8, one launch (start us, length us, event | category | flops | bytes accessed | tf_op | source)
XLA Modules:
  0.0 609.2 jit_solution(3356555167298708479)
XLA Ops:
  9.3 6.7 %collective-permute-done = f32[16,6,8,128]{3,1,2,0:T(8,128)S(1)} collective-permute-done((f32[16,6,8,128]{3,1,2,0:T(8,128)S(1)}, f32[16,6,8,128]{3,1,2,0:T(8,128)S(1)}, u32[]{:S(2)}, u32[]{:S(2)}) %collective-permute-start) | collective-permute-done | bytes 393248 | tf_op jit(solution)/shard_map/ppermute | solution.py:24
  17.9 8.1 %collective-permute-start.1 = (f32[16,16,6,128]{3,1,2,0:T(8,128)S(1)}, f32[16,16,6,128]{3,1,2,0:T(8,128)S(1)}, u32[]{:S(2)}, u32[]{:S(2)}) collective-permute-start(f32[16,16,6,128]{3,1,2,0:T(8,128)S(1)} %slice.105), channel_id=1, source_target_pairs={{0,31},{1,0},{2,1},{3,2},{4,3},{5,4},{6,5},{7,6},{8,7},{9,8},{10,9... | collective-permute-start | bytes 2359304 | tf_op jit(solution)/shard_map/ppermute | solution.py:24
  26.0 17.1 %collective-permute-done.1 = f32[16,16,6,128]{3,1,2,0:T(8,128)S(1)} collective-permute-done((f32[16,16,6,128]{3,1,2,0:T(8,128)S(1)}, f32[16,16,6,128]{3,1,2,0:T(8,128)S(1)}, u32[]{:S(2)}, u32[]{:S(2)}) %collective-permute-start.1) | collective-permute-done | bytes 786464 | tf_op jit(solution)/shard_map/ppermute | solution.py:24
  54.1 7.6 %all-to-all-start = ((f32[32,1,4096]{2,1,0:T(1,128)}), f32[32,1,4096]{2,1,0:T(1,128)S(1)}, u32[]{:S(2)}, u32[]{:S(2)}) async-start(f32[32,1,4096]{2,1,0:T(1,128)} %reshape.86), calls=%async_computation | async-start | bytes 1048576 | tf_op jit(solution)/shard_map/all_to_all | solution.py:127
  61.7 6.2 %copy.304 = f32[4,16,16,256]{2,1,3,0:T(8,128)} copy(f32[4,16,16,256]{3,2,1,0:T(8,128)S(1)} %copy-done.4) | data formatting | bytes 2097152 | tf_op jit(solution)/shard_map/reshape | solution.py:188
  68.0 11.4 %all-to-all-done = f32[32,1,4096]{2,1,0:T(1,128)S(1)} async-done(((f32[32,1,4096]{2,1,0:T(1,128)}), f32[32,1,4096]{2,1,0:T(1,128)S(1)}, u32[]{:S(2)}, u32[]{:S(2)}) %all-to-all-start) | async-done | bytes 524320 | tf_op jit(solution)/shard_map/all_to_all | solution.py:127
  105.0 14.3 %all_gather.6 = f32[64,32,32]{0,2,1:T(8,128)S(1)} all-gather(f32[64,4,32]{0,2,1:T(8,128)S(1)} %fusion.123), channel_id=1, replica_groups=mesh['gx'=8,'gy'=32] {'gx'}, dimensions={1}, use_global_device_ids=true | all-gather | bytes 294912 | tf_op jit(solution)/shard_map/all_gather | solution.py:142
  125.7 14.9 %bitcast_subtract_fusion.1 = f32[4,16,4,16,16]{1,2,4,3,0:T(4,128)S(1)} fusion(f32[4,16,16,16,16]{2,1,4,3,0:T(8,128)} %bitcast.264, f32[1,16,4,16,16]{1,2,4,3,0:T(4,128)S(1)} %copy.227, f32[1,16,4,16,16]{1,2,4,3,0:T(4,128)S(1)} %copy.226, f32[1,16,4,16,16]{1,2,4,3,0:T(4,128)S(1)} %copy.225, f32[1,16,4,16,16]{1,2,4,3,0:T(4,128)S(1)} %copy.224), kind=kOutput, calls=%fused_computation.23 | convolution fusion | flops 13041664 | bytes 1572864 | tf_op jit(solution)/shard_map/bizxy,bioxy->bozxy/dot_general | solution.py:151
  175.0 22.0 %all_to_all.72 = f32[32,1,4096]{2,1,0:T(1,128)S(1)} all-to-all(f32[32,1,4096]{2,1,0:T(1,128)S(1)} %reshape.88), channel_id=1, replica_groups=mesh['gx'=8,'gy'=32] {'gy'}, dimensions={0} | all-to-all | bytes 1048576 | tf_op jit(solution)/shard_map/all_to_all | solution.py:168
  220.1 15.0 %collective-permute-done.7 = f32[16,32,3,128]{3,1,2,0:T(8,128)S(1)} collective-permute-done((f32[16,32,3,128]{3,1,2,0:T(8,128)S(1)}, f32[16,32,3,128]{3,1,2,0:T(8,128)S(1)}, u32[]{:S(2)}, u32[]{:S(2)}) %collective-permute-start.7) | collective-permute-done | bytes 786464 | tf_op jit(solution)/shard_map/ppermute | solution.py:24
  235.3 6.6 %fusion.1133 = (f32[16]{0:T(128)}, f32[16,32,8,128]{3,2,1,0:T(8,128)S(1)}, f32[16,32,8,128]{3,2,1,0:T(8,128)}) fusion(f32[16,32,8,128]{3,2,1,0:T(8,128)S(1)} %copy-done.20, f32[16]{0:T(128)S(1)} %copy-done.21, f32[16,32,8,128]{3,0,2,1:T(8,128)S(1)} %fusion.27, f32[16,32,8,128]{3,2,1,0:T(8,128)S(1)} %copy-done.1, s32[7]{0:T(128)S(1)} %iota_multiply_fusion.2, ...), kind=kOutput, calls=%fused_computation.1198 | convolution fusion | flops 56100200 | bytes 12320924 | tf_op jit(solution)/shard_map/kr,axrs->axks/dot_general | solution.py:54
  241.9 5.3 collective-permute-done.8
  249.6 19.6 %collective-permute-done.9 = f32[16,16,6,128]{3,1,2,0:T(8,128)S(1)} collective-permute-done((f32[16,16,6,128]{3,1,2,0:T(8,128)S(1)}, f32[16,16,6,128]{3,1,2,0:T(8,128)S(1)}, u32[]{:S(2)}, u32[]{:S(2)}) %collective-permute-start.9) | collective-permute-done | bytes 786464 | tf_op jit(solution)/shard_map/ppermute | solution.py:24
  279.4 19.5 %all_to_all.73 = f32[32,1,4096]{2,1,0:T(1,128)S(1)} all-to-all(f32[32,1,4096]{2,1,0:T(1,128)S(1)} %reshape.90), channel_id=1, replica_groups=mesh['gx'=8,'gy'=32] {'gy'}, dimensions={0} | all-to-all | bytes 1048576 | tf_op jit(solution)/shard_map/all_to_all | solution.py:127
  319.1 5.1 collective-permute-done.11
  325.1 17.3 %all_gather.7 = f32[64,32,32]{0,2,1:T(8,128)S(1)} all-gather(f32[64,4,32]{0,2,1:T(8,128)S(1)} %fusion.119), channel_id=1, replica_groups=mesh['gx'=8,'gy'=32] {'gx'}, dimensions={1}, use_global_device_ids=true | all-gather | bytes 294912 | tf_op jit(solution)/shard_map/all_gather | solution.py:142
  350.4 18.2 %bitcast_subtract_fusion = f32[4,16,4,16,16]{1,2,4,3,0:T(4,128)S(1)} fusion(f32[4,16,16,16,16]{2,1,4,3,0:T(8,128)} %bitcast.265, f32[1,16,4,16,16]{1,2,4,3,0:T(4,128)} %copy.269, f32[1,16,4,16,16]{1,2,4,3,0:T(4,128)} %copy.268, f32[1,16,4,16,16]{1,2,4,3,0:T(4,128)} %copy.267, f32[1,16,4,16,16]{1,2,4,3,0:T(4,128)S(1)} %copy.266), kind=kOutput, calls=%fused_computation.19 | convolution fusion | flops 13041664 | bytes 1572864 | tf_op jit(solution)/shard_map/bozxy,bioxy->bizxy/dot_general | solution.py:147
  409.7 5.7 all-to-all-start.3
  415.5 17.6 %fusion.86 = f32[4,16,16,16,16]{4,3,2,1,0:T(8,128)} fusion(f32[1,16,4,16,16]{1,2,4,3,0:T(4,128)} %copy.269, f32[1,16,4,16,16]{1,2,4,3,0:T(4,128)} %copy.268, f32[1,16,4,16,16]{1,2,4,3,0:T(4,128)} %copy.267, f32[1,16,4,16,16]{1,2,4,3,0:T(4,128)} %copy-done.10, f32[1,16,4,16,16]{1,2,4,3,0:T(4,128)} %copy-done.9, f32[1,16,4,16,16]{1,2,4,3,0:T(4,128)} %copy-done.7, ...), kind=kOutput, calls=%fused_computation.106 | convolution fusion | flops 12976128 | bytes 1572864 | tf_op jit(solution)/shard_map/bizxy,bozxy->bioxy/dot_general | solution.py:201
  433.0 7.7 %copy.290 = f32[4,16,16,256]{3,2,1,0:T(8,128)} copy(f32[4,16,16,256]{1,2,3,0:T(8,128)} %bitcast.266) | data formatting | bytes 2097152 | tf_op jit(solution)/shard_map/reshape | solution.py:204
  440.8 6.3 %fusion.45 = f32[16,16]{0,1:T(8,128)S(1)} fusion(f32[16,32,8,128]{3,2,1,0:T(8,128)} %param.5, f32[16,32,8,128]{3,2,1,0:T(8,128)S(1)} %get-tuple-element.28), kind=kOutput, calls=%fused_computation.66 | convolution fusion | flops 100663296 | bytes 4195328 | tf_op jit(solution)/shard_map/ixys,oxys->io/dot_general | solution.py:206
  447.1 77.5 %all-reduce = (f32[16,16]{0,1:T(8,128)S(1)}, f32[16]{0:T(128)S(1)}) all-reduce(f32[16,16]{0,1:T(8,128)S(1)} %fusion.45, f32[16]{0:T(128)S(1)} %copy-done.19), channel_id=1, replica_groups=mesh['gx'=8,'gy'=32] {'gx','gy'}, use_global_device_ids=true, to_apply=%region_1.2 | all-reduce | flops 272 | bytes 2176 | tf_op jit(solution)/shard_map/psum | solution.py:210
  551.4 41.4 %all-reduce.3.cloned.1.call-done = f32[4,16,16,256]{3,2,1,0:T(8,128)} async-done(((f32[4,16,16,256]{3,2,1,0:T(8,128)}), f32[4,16,16,256]{3,2,1,0:T(8,128)}) %all-reduce.3.cloned.1.call-update) | async-done | bytes 1048592 | tf_op jit(solution)/shard_map/psum | solution.py:205
  596.9 5.2 bitcast_add_fusion
  (209 shorter events, 217.6 us)
Async XLA Ops:
  7.2 210.0 %copy-start = (f32[16,16]{1,0:T(8,128)S(1)}, f32[16,16]{1,0:T(8,128)}, u32[]{:S(2)}) copy-start(f32[16,16]{1,0:T(8,128)} %param.8) | copy-start | bytes 3076
  9.2 6.7 %collective-permute-start = (f32[16,6,8,128]{3,1,2,0:T(8,128)S(1)}, f32[16,6,8,128]{3,1,2,0:T(8,128)S(1)}, u32[]{:S(2)}, u32[]{:S(2)}) collective-permute-start(f32[16,6,8,128]{3,1,2,0:T(8,128)S(1)} %slice.104), channel_id=1, source_target_pairs={{0,224},{32,0},{64,32},{96,64},{128,96},{160,128},{192,160},{224,1... | collective-permute-start | bytes 1179656 | tf_op jit(solution)/shard_map/ppermute | solution.py:24
  17.9 25.2 %collective-permute-start.1 = (f32[16,16,6,128]{3,1,2,0:T(8,128)S(1)}, f32[16,16,6,128]{3,1,2,0:T(8,128)S(1)}, u32[]{:S(2)}, u32[]{:S(2)}) collective-permute-start(f32[16,16,6,128]{3,1,2,0:T(8,128)S(1)} %slice.105), channel_id=1, source_target_pairs={{0,31},{1,0},{2,1},{3,2},{4,3},{5,4},{6,5},{7,6},{8,7},{9,8},{10,9... | collective-permute-start | bytes 2359304 | tf_op jit(solution)/shard_map/ppermute | solution.py:24
  54.1 25.3 %all-to-all-start = ((f32[32,1,4096]{2,1,0:T(1,128)}), f32[32,1,4096]{2,1,0:T(1,128)S(1)}, u32[]{:S(2)}, u32[]{:S(2)}) async-start(f32[32,1,4096]{2,1,0:T(1,128)} %reshape.86), calls=%async_computation | async-start | bytes 1048576 | tf_op jit(solution)/shard_map/all_to_all | solution.py:127
  93.2 3.9 collective-permute-start.2
  98.2 5.8 collective-permute-start.3
  100.1 224.6 %copy-start.15 = (s32[32]{0:T(128)}, s32[32]{0:T(128)S(1)}, u32[]{:S(2)}) copy-start(s32[32]{0:T(128)S(1)} %iota_multiply_fusion.3) | copy-start | bytes 388
  150.8 5.0 collective-permute-start.4
  150.9 84.3 %copy-start.11 = (s32[7]{0:T(128)}, s32[7]{0:T(128)S(1)}, u32[]{:S(2)}) copy-start(s32[7]{0:T(128)S(1)} %iota_multiply_fusion.2) | copy-start | bytes 88
  156.7 4.1 collective-permute-start.5
  209.3 4.4 collective-permute-start.6
  214.9 20.2 %collective-permute-start.7 = (f32[16,32,3,128]{3,1,2,0:T(8,128)S(1)}, f32[16,32,3,128]{3,1,2,0:T(8,128)S(1)}, u32[]{:S(2)}, u32[]{:S(2)}) collective-permute-start(f32[16,32,3,128]{3,1,2,0:T(8,128)S(1)} %slice.115), channel_id=1, source_target_pairs={{0,1},{1,2},{2,3},{3,4},{4,5},{5,6},{6,7},{7,8},{8,9},{9,10},{10,1... | collective-permute-start | bytes 2359304 | tf_op jit(solution)/shard_map/ppermute | solution.py:24
  220.0 15.2 %copy-start.20 = (f32[16,32,8,128]{3,2,1,0:T(8,128)S(1)}, f32[16,32,8,128]{3,2,1,0:T(8,128)}, u32[]{:S(2)}) copy-start(f32[16,32,8,128]{3,2,1,0:T(8,128)} %param.6) | copy-start | bytes 6291460
  220.0 15.2 %copy-start.21 = (f32[16]{0:T(128)S(1)}, f32[16]{0:T(128)}, u32[]{:S(2)}) copy-start(f32[16]{0:T(128)} %param.9) | copy-start | bytes 196
  241.9 5.3 collective-permute-start.8
  249.5 19.7 %collective-permute-start.9 = (f32[16,16,6,128]{3,1,2,0:T(8,128)S(1)}, f32[16,16,6,128]{3,1,2,0:T(8,128)S(1)}, u32[]{:S(2)}, u32[]{:S(2)}) collective-permute-start(f32[16,16,6,128]{3,1,2,0:T(8,128)S(1)} %slice.117), channel_id=1, source_target_pairs={{0,31},{1,0},{2,1},{3,2},{4,3},{5,4},{6,5},{7,6},{8,7},{9,8},{10,9... | collective-permute-start | bytes 2359304 | tf_op jit(solution)/shard_map/ppermute | solution.py:24
  312.2 3.9 collective-permute-start.10
  317.2 7.0 %collective-permute-start.11 = (f32[64,6,64]{2,1,0:T(8,128)S(1)}, f32[64,6,64]{2,1,0:T(8,128)S(1)}, u32[]{:S(2)}, u32[]{:S(2)}) collective-permute-start(f32[64,6,64]{2,1,0:T(8,128)S(1)} %bitcast.290), channel_id=1, source_target_pairs={{0,224},{32,0},{64,32},{96,64},{128,96},{160,128},{192,160},{224,1... | collective-permute-start | bytes 294920 | tf_op jit(solution)/shard_map/ppermute | solution.py:24
  384.8 5.0 collective-permute-start.12
  390.7 4.1 collective-permute-start.13
  409.7 114.9 %all-to-all-start.3 = ((f32[32,1,4096]{2,1,0:T(1,128)}), f32[32,1,4096]{2,1,0:T(1,128)S(1)}, u32[]{:S(2)}, u32[]{:S(2)}) async-start(f32[32,1,4096]{2,1,0:T(1,128)} %reshape.92), calls=%async_computation.3 | async-start | bytes 1048576 | tf_op jit(solution)/shard_map/all_to_all | solution.py:168
  415.4 177.4 %all-reduce.3.cloned.1.call-start = ((), (), s32[]{:S(2)}) async-start(), calls=%async_computation.4 | async-start | bytes 2097152 | tf_op jit(solution)/shard_map/psum | solution.py:205
  536.9 4.9 collective-permute-start.14
  545.0 50.1 %collective-permute-start.15 = (f32[16,32,3,128]{3,1,2,0:T(8,128)}, f32[16,32,3,128]{3,1,2,0:T(8,128)}, u32[]{:S(2)}, u32[]{:S(2)}) collective-permute-start(f32[16,32,3,128]{3,1,2,0:T(8,128)} %slice.127), channel_id=1, source_target_pairs={{0,1},{1,2},{2,3},{3,4},{4,5},{5,6},{6,7},{7,8},{8,9},{9,10},{10,1... | collective-permute-start | bytes 2359304 | tf_op jit(solution)/shard_map/ppermute | solution.py:24
  (17 other events, 111.1 us)
Sparse Core Ops, SparseCore 0:
  440.9 151.8 all-reduce.2
where the time goes:
time: 616 us; the launch traced here: 609 us
  waiting for transfers between devices  159 us (26%)
  blocking collectives  151 us (25%)
  local copies, waits for them, and re-layouts  122 us (20%)
  matrix products  119 us (19%)
  starting transfers between devices  29.7 us (5%)
  between operations  15.3 us (2%)
  other arithmetic  13.7 us (2%)
    ppermute x16, waiting for transfers between devices, from_behind(): lax.ppermute(value, axis, [(i, (i + by) % devices) for i in range(devices)])  106 us
    psum x1, blocking collectives, local(): point_total, bias_total = lax.psum((point_local, bias_local), ('gx', 'gy'))  77.5 us
    psum x1, waiting for transfers between devices, local(): mode_total = lax.psum(mode_local, 'gy')  41.4 us
    unnamed x56, local copies, waits for them, and re-layouts  40.1 us
    all_gather x2, blocking collectives, wave_block(): gathered = lax.all_gather(level_three, 'gx', axis=1, tiled=True)  31.6 us
    all_to_all x1, blocking collectives, wave_block(): lax.all_to_all(from_lanes(delta_one, channels), 'gy', split_axis=2, conca...  22 us
    dot_general x24, matrix products, plane_y(): jnp.einsum('kr,axr->axk', matrix, signal, precision=lax.Precision.HIGHEST)  20.3 us
    all_to_all x1, blocking collectives, wave_block(): lax.all_to_all(level_one, 'gy', split_axis=3, concat_axis=2, tiled=True)  19.5 us
  transfers between devices with their start and end apart: 19, of which 17 were waited for; matrix products, arithmetic and copies ran while one was open for 11% of the time, Pallas kernels for 0%

commit v1 on v0

--- a/solution.py
+++ b/solution.py
@@ -17,6 +17,16 @@
 HIGH_PASS = [(-1) ** position * LOW_PASS[7 - position] for position in range(8)]
 GELU_SCALE = 0.7978845608028654
 GELU_CUBE = 0.044715
+
+
+def feed_clusters(mine, group_axis):
+    axis_n = lax.axis_size(group_axis)
+    res, g_now = (mine, 0)
+    while 1 << g_now < axis_n:
+        before = lax.ppermute(res, group_axis, [(m, m ^ 1 << g_now) for m in range(axis_n)])
+        res = res + before
+        g_now = g_now + 1
+    return res
 
 
 def from_behind(value, axis, by):
@@ -202,7 +212,7 @@
         "bizxy,bozxy->bioxy", bands_flow, bands_grad, precision=lax.Precision.HIGHEST
     )
     mode_local = mode_local.reshape(4, channels, channels, modes_x * modes_y)
-    mode_total = lax.psum(mode_local, "gy")
+    mode_total = feed_clusters(mode_local, "gy")
     point_local = jnp.einsum(
         "ixys,oxys->io", flow_field, grad_inner, precision=lax.Precision.HIGHEST
     )

time: 616 us -> 678 us (1.10)
  waiting for transfers between devices: 159 us -> 206 us
  between operations: 15.3 us -> 2.15 us
  starting transfers between devices: 29.7 us -> 39.7 us
  other arithmetic: 13.7 us -> 21.1 us
    ppermute x0 -> x5, waiting for transfers between devices: none -> 87.7 us  [feed_clusters(): lax.ppermute(res, group_axis, [(m, m ^ 1 << g_now) for m in range(axis_n)])]
    psum x1 -> x0, waiting for transfers between devices: 41.4 us -> none  [local(): mode_total = lax.psum(mode_local, 'gy')]
    ppermute x0 -> x5, starting transfers between devices: none -> 8.77 us  [feed_clusters(): lax.ppermute(res, group_axis, [(m, m ^ 1 << g_now) for m in range(axis_n)])]
    add x0 -> x4, other arithmetic: none -> 8.41 us  [feed_clusters(): res = res + before]
    unnamed x56 -> x66, local copies, waits for them, and re-layouts: 40.1 us -> 40.6 us
  transfers between devices with their start and end apart: 19 -> 23, of which waited for: 17 -> 20; matrix products, arithmetic and copies ran while one was open for 11% -> 13% of each run, Pallas kernels for 0% -> 0%
where the time goes in v1:
time: 678 us; the launch traced here: 670 us
  waiting for transfers between devices  206 us (30%)
  blocking collectives  154 us (23%)
  local copies, waits for them, and re-layouts  127 us (19%)
  matrix products  120 us (18%)
  starting transfers between devices  39.7 us (6%)
  other arithmetic  21.1 us (3%)
    ppermute x16, waiting for transfers between devices, from_behind(): lax.ppermute(value, axis, [(i, (i + by) % devices) for i in range(devices)])  101 us
    ppermute x5, waiting for transfers between devices, feed_clusters(): lax.ppermute(res, group_axis, [(m, m ^ 1 << g_now) for m in range(axis_n)])  87.7 us
    psum x1, blocking collectives, local(): point_total, bias_total = lax.psum((point_local, bias_local), ('gx', 'gy'))  80.7 us
    unnamed x66, local copies, waits for them, and re-layouts  40.6 us
    all_gather x2, blocking collectives, wave_block(): gathered = lax.all_gather(level_three, 'gx', axis=1, tiled=True)  31.6 us
    dot_general x24, matrix products, plane_y(): jnp.einsum('kr,axr->axk', matrix, signal, precision=lax.Precision.HIGHEST)  22.5 us
    all_to_all x1, blocking collectives, wave_block(): lax.all_to_all(from_lanes(delta_one, channels), 'gy', split_axis=2, conca...  22.1 us
    dot_general x1, matrix products, wave_block(): jnp.einsum('bozxy,bioxy->bizxy', split_bands, weights_grid, precision=lax...  20.2 us
  transfers between devices with their start and end apart: 23, of which 20 were waited for; matrix products, arithmetic and copies ran while one was open for 13% of the time, Pallas kernels for 0%

profile of v1, /device:TPU:8, one launch (start us, length us, event | category | flops | bytes accessed | tf_op | source)
XLA Modules:
  0.0 670.0 jit_solution(13528114457484593911)
XLA Ops:
  2.7 6.7 collective-permute-done
  11.3 8.1 %collective-permute-start.1 = (f32[16,16,6,128]{3,1,2,0:T(8,128)S(1)}, f32[16,16,6,128]{3,1,2,0:T(8,128)S(1)}, u32[]{:S(2)}, u32[]{:S(2)}) collective-permute-start(f32[16,16,6,128]{3,1,2,0:T(8,128)S(1)} %slice.105), channel_id=1, source_target_pairs={{0,31},{1,0},{2,1},{3,2},{4,3},{5,4},{6,5},{7,6},{8,7},{9,8},{10,9... | collective-permute-start | bytes 2359304 | tf_op jit(solution)/shard_map/ppermute | solution.py:34
  19.5 17.1 %collective-permute-done.1 = f32[16,16,6,128]{3,1,2,0:T(8,128)S(1)} collective-permute-done((f32[16,16,6,128]{3,1,2,0:T(8,128)S(1)}, f32[16,16,6,128]{3,1,2,0:T(8,128)S(1)}, u32[]{:S(2)}, u32[]{:S(2)}) %collective-permute-start.1) | collective-permute-done | bytes 786464 | tf_op jit(solution)/shard_map/ppermute | solution.py:34
  47.6 7.7 %all-to-all-start = ((f32[32,1,4096]{2,1,0:T(1,128)}), f32[32,1,4096]{2,1,0:T(1,128)S(1)}, u32[]{:S(2)}, u32[]{:S(2)}) async-start(f32[32,1,4096]{2,1,0:T(1,128)} %reshape.86), calls=%async_computation | async-start | bytes 1048576 | tf_op jit(solution)/shard_map/all_to_all | solution.py:137
  55.3 6.2 copy.308
  61.5 11.4 %all-to-all-done = f32[32,1,4096]{2,1,0:T(1,128)S(1)} async-done(((f32[32,1,4096]{2,1,0:T(1,128)}), f32[32,1,4096]{2,1,0:T(1,128)S(1)}, u32[]{:S(2)}, u32[]{:S(2)}) %all-to-all-start) | async-done | bytes 524320 | tf_op jit(solution)/shard_map/all_to_all | solution.py:137
  98.5 14.5 %all_gather.6 = f32[64,32,32]{0,2,1:T(8,128)S(1)} all-gather(f32[64,4,32]{0,2,1:T(8,128)S(1)} %fusion.123), channel_id=1, replica_groups=mesh['gx'=8,'gy'=32] {'gx'}, dimensions={1}, use_global_device_ids=true | all-gather | bytes 294912 | tf_op jit(solution)/shard_map/all_gather | solution.py:152
  119.4 14.6 %bitcast_subtract_fusion.1 = f32[4,16,4,16,16]{1,2,4,3,0:T(4,128)S(1)} fusion(f32[4,16,16,16,16]{2,1,4,3,0:T(8,128)} %bitcast.264, f32[1,16,4,16,16]{1,2,4,3,0:T(4,128)S(1)} %copy.230, f32[1,16,4,16,16]{1,2,4,3,0:T(4,128)S(1)} %copy.229, f32[1,16,4,16,16]{1,2,4,3,0:T(4,128)S(1)} %copy.228, f32[1,16,4,16,16]{1,2,4,3,0:T(4,128)S(1)} %copy.227), kind=kOutput, calls=%fused_computation.23 | convolution fusion | flops 13041664 | bytes 1572864 | tf_op jit(solution)/shard_map/bizxy,bioxy->bozxy/dot_general | solution.py:161
  168.6 22.1 %all_to_all.72 = f32[32,1,4096]{2,1,0:T(1,128)S(1)} all-to-all(f32[32,1,4096]{2,1,0:T(1,128)S(1)} %reshape.88), channel_id=1, replica_groups=mesh['gx'=8,'gy'=32] {'gy'}, dimensions={0} | all-to-all | bytes 1048576 | tf_op jit(solution)/shard_map/all_to_all | solution.py:178
  213.7 15.0 %collective-permute-done.7 = f32[16,32,3,128]{3,1,2,0:T(8,128)S(1)} collective-permute-done((f32[16,32,3,128]{3,1,2,0:T(8,128)S(1)}, f32[16,32,3,128]{3,1,2,0:T(8,128)S(1)}, u32[]{:S(2)}, u32[]{:S(2)}) %collective-permute-start.7) | collective-permute-done | bytes 786464 | tf_op jit(solution)/shard_map/ppermute | solution.py:34
  229.0 6.8 %fusion.1133 = (f32[16]{0:T(128)}, f32[16,32,8,128]{3,2,1,0:T(8,128)S(1)}, f32[16,32,8,128]{3,2,1,0:T(8,128)}) fusion(f32[16,32,8,128]{3,2,1,0:T(8,128)S(1)} %copy-done.25, f32[16]{0:T(128)S(1)} %copy-done.26, f32[16,32,8,128]{3,0,2,1:T(8,128)S(1)} %fusion.27, f32[16,32,8,128]{3,2,1,0:T(8,128)S(1)} %copy-done.1, s32[7]{0:T(128)S(1)} %iota_multiply_fusion.2, ...), kind=kOutput, calls=%fused_computation.1198 | convolution fusion | flops 56100200 | bytes 12320924 | tf_op jit(solution)/shard_map/kr,axrs->axks/dot_general | solution.py:64
  235.8 5.3 collective-permute-done.8
  243.5 19.6 %collective-permute-done.9 = f32[16,16,6,128]{3,1,2,0:T(8,128)S(1)} collective-permute-done((f32[16,16,6,128]{3,1,2,0:T(8,128)S(1)}, f32[16,16,6,128]{3,1,2,0:T(8,128)S(1)}, u32[]{:S(2)}, u32[]{:S(2)}) %collective-permute-start.9) | collective-permute-done | bytes 786464 | tf_op jit(solution)/shard_map/ppermute | solution.py:34
  273.3 19.4 %all_to_all.73 = f32[32,1,4096]{2,1,0:T(1,128)S(1)} all-to-all(f32[32,1,4096]{2,1,0:T(1,128)S(1)} %reshape.90), channel_id=1, replica_groups=mesh['gx'=8,'gy'=32] {'gy'}, dimensions={0} | all-to-all | bytes 1048576 | tf_op jit(solution)/shard_map/all_to_all | solution.py:137
  319.1 17.2 %all_gather.7 = f32[64,32,32]{0,2,1:T(8,128)S(1)} all-gather(f32[64,4,32]{0,2,1:T(8,128)S(1)} %fusion.119), channel_id=1, replica_groups=mesh['gx'=8,'gy'=32] {'gx'}, dimensions={1}, use_global_device_ids=true | all-gather | bytes 294912 | tf_op jit(solution)/shard_map/all_gather | solution.py:152
  345.0 17.7 %fusion.86 = f32[4,16,16,16,16]{4,3,2,1,0:T(8,128)} fusion(f32[1,16,4,16,16]{1,2,4,3,0:T(4,128)} %copy.272, f32[1,16,4,16,16]{1,2,4,3,0:T(4,128)} %copy.271, f32[1,16,4,16,16]{1,2,4,3,0:T(4,128)} %copy.270, f32[1,16,4,16,16]{1,2,4,3,0:T(4,128)} %copy.269, f32[1,16,4,16,16]{1,2,4,3,0:T(4,128)} %copy-done.11, f32[1,16,4,16,16]{1,2,4,3,0:T(4,128)} %copy-done.9, ...), kind=kOutput, calls=%fused_computation.106 | convolution fusion | flops 12976128 | bytes 1572864 | tf_op jit(solution)/shard_map/bizxy,bozxy->bioxy/dot_general | solution.py:211
  362.7 20.2 %bitcast_subtract_fusion = f32[4,16,4,16,16]{1,2,4,3,0:T(4,128)} fusion(f32[4,16,16,16,16]{2,1,4,3,0:T(8,128)} %bitcast.265, f32[1,16,4,16,16]{1,2,4,3,0:T(4,128)S(1)} %copy-done.15, f32[1,16,4,16,16]{1,2,4,3,0:T(4,128)S(1)} %copy-done.13, f32[1,16,4,16,16]{1,2,4,3,0:T(4,128)S(1)} %copy-done.14, f32[1,16,4,16,16]{1,2,4,3,0:T(4,128)S(1)} %copy-done.12), kind=kOutput, calls=%fused_computation.19 | convolution fusion | flops 13041664 | bytes 1572864 | tf_op jit(solution)/shard_map/bozxy,bioxy->bizxy/dot_general | solution.py:157
  383.0 6.5 copy.294
  431.5 36.4 %collective-permute-done.17 = f32[4,16,16,256]{3,2,1,0:T(8,128)} collective-permute-done((f32[4,16,16,256]{3,2,1,0:T(8,128)}, f32[4,16,16,256]{3,2,1,0:T(8,128)}, u32[]{:S(2)}, u32[]{:S(2)}) %collective-permute-start.17) | collective-permute-done | bytes 1048608 | tf_op jit(solution)/shard_map/ppermute | solution.py:26
  480.3 7.2 %all-to-all-start.3 = ((f32[32,1,4096]{2,1,0:T(1,128)}), f32[32,1,4096]{2,1,0:T(1,128)}, u32[]{:S(2)}, u32[]{:S(2)}) async-start(f32[32,1,4096]{2,1,0:T(1,128)} %reshape.92), calls=%async_computation.3 | async-start | bytes 1048576 | tf_op jit(solution)/shard_map/all_to_all | solution.py:178
  487.5 35.5 %collective-permute-done.18 = f32[4,16,16,256]{3,2,1,0:T(8,128)} collective-permute-done((f32[4,16,16,256]{3,2,1,0:T(8,128)S(1)}, f32[4,16,16,256]{3,2,1,0:T(8,128)}, u32[]{:S(2)}, u32[]{:S(2)}) %collective-permute-start.18) | collective-permute-done | bytes 1048608 | tf_op jit(solution)/shard_map/ppermute | solution.py:26
  526.1 5.9 all-to-all-done.3
  558.8 80.7 %all-reduce = (f32[16,16]{0,1:T(8,128)S(1)}, f32[16]{0:T(128)S(1)}) all-reduce(f32[16,16]{0,1:T(8,128)S(1)} %fusion.45, f32[16]{0:T(128)S(1)} %copy-done.24), channel_id=1, replica_groups=mesh['gx'=8,'gy'=32] {'gx','gy'}, use_global_device_ids=true, to_apply=%region_0.1 | all-reduce | flops 272 | bytes 2176 | tf_op jit(solution)/shard_map/psum | solution.py:220
  654.0 14.4 %collective-permute-done.20 = f32[4,16,16,256]{3,2,1,0:T(8,128)S(1)} collective-permute-done((f32[4,16,16,256]{3,2,1,0:T(8,128)S(1)}, f32[4,16,16,256]{3,2,1,0:T(8,128)S(1)}, u32[]{:S(2)}, u32[]{:S(2)}) %collective-permute-start.20) | collective-permute-done | bytes 1048608 | tf_op jit(solution)/shard_map/ppermute | solution.py:26
  (230 shorter events, 251.7 us)
Async XLA Ops:
  2.7 6.7 %collective-permute-start = (f32[16,6,8,128]{3,1,2,0:T(8,128)S(1)}, f32[16,6,8,128]{3,1,2,0:T(8,128)S(1)}, u32[]{:S(2)}, u32[]{:S(2)}) collective-permute-start(f32[16,6,8,128]{3,1,2,0:T(8,128)S(1)} %slice.104), channel_id=1, source_target_pairs={{0,224},{32,0},{64,32},{96,64},{128,96},{160,128},{192,160},{224,1... | collective-permute-start | bytes 1179656 | tf_op jit(solution)/shard_map/ppermute | solution.py:34
  11.3 25.2 %collective-permute-start.1 = (f32[16,16,6,128]{3,1,2,0:T(8,128)S(1)}, f32[16,16,6,128]{3,1,2,0:T(8,128)S(1)}, u32[]{:S(2)}, u32[]{:S(2)}) collective-permute-start(f32[16,16,6,128]{3,1,2,0:T(8,128)S(1)} %slice.105), channel_id=1, source_target_pairs={{0,31},{1,0},{2,1},{3,2},{4,3},{5,4},{6,5},{7,6},{8,7},{9,8},{10,9... | collective-permute-start | bytes 2359304 | tf_op jit(solution)/shard_map/ppermute | solution.py:34
  47.6 25.3 %all-to-all-start = ((f32[32,1,4096]{2,1,0:T(1,128)}), f32[32,1,4096]{2,1,0:T(1,128)S(1)}, u32[]{:S(2)}, u32[]{:S(2)}) async-start(f32[32,1,4096]{2,1,0:T(1,128)} %reshape.86), calls=%async_computation | async-start | bytes 1048576 | tf_op jit(solution)/shard_map/all_to_all | solution.py:137
  86.7 3.9 collective-permute-start.2
  91.7 5.8 collective-permute-start.3
  93.6 225.0 %copy-start.20 = (s32[32]{0:T(128)}, s32[32]{0:T(128)S(1)}, u32[]{:S(2)}) copy-start(s32[32]{0:T(128)S(1)} %iota_multiply_fusion.3) | copy-start | bytes 388
  144.3 5.0 collective-permute-start.4
  150.2 4.1 collective-permute-start.5
  203.0 4.4 collective-permute-start.6
  208.6 20.2 %collective-permute-start.7 = (f32[16,32,3,128]{3,1,2,0:T(8,128)S(1)}, f32[16,32,3,128]{3,1,2,0:T(8,128)S(1)}, u32[]{:S(2)}, u32[]{:S(2)}) collective-permute-start(f32[16,32,3,128]{3,1,2,0:T(8,128)S(1)} %slice.115), channel_id=1, source_target_pairs={{0,1},{1,2},{2,3},{3,4},{4,5},{5,6},{6,7},{7,8},{8,9},{9,10},{10,1... | collective-permute-start | bytes 2359304 | tf_op jit(solution)/shard_map/ppermute | solution.py:34
  235.8 5.3 collective-permute-start.8
  243.4 19.7 %collective-permute-start.9 = (f32[16,16,6,128]{3,1,2,0:T(8,128)S(1)}, f32[16,16,6,128]{3,1,2,0:T(8,128)S(1)}, u32[]{:S(2)}, u32[]{:S(2)}) collective-permute-start(f32[16,16,6,128]{3,1,2,0:T(8,128)S(1)} %slice.117), channel_id=1, source_target_pairs={{0,31},{1,0},{2,1},{3,2},{4,3},{5,4},{6,5},{7,6},{8,7},{9,8},{10,9... | collective-permute-start | bytes 2359304 | tf_op jit(solution)/shard_map/ppermute | solution.py:34
  306.0 3.9 collective-permute-start.10
  311.0 7.1 %collective-permute-start.11 = (f32[64,6,64]{2,1,0:T(8,128)S(1)}, f32[64,6,64]{2,1,0:T(8,128)S(1)}, u32[]{:S(2)}, u32[]{:S(2)}) collective-permute-start(f32[64,6,64]{2,1,0:T(8,128)S(1)} %bitcast.290), channel_id=1, source_target_pairs={{0,224},{32,0},{64,32},{96,64},{128,96},{160,128},{192,160},{224,1... | collective-permute-start | bytes 294920 | tf_op jit(solution)/shard_map/ppermute | solution.py:34
  389.5 26.6 %collective-permute-start.16 = (f32[4,16,16,256]{3,2,1,0:T(8,128)S(1)}, f32[4,16,16,256]{3,2,1,0:T(8,128)}, u32[]{:S(2)}, u32[]{:S(2)}) collective-permute-start(f32[4,16,16,256]{3,2,1,0:T(8,128)S(1)} %copy.294), channel_id=1, source_target_pairs={{0,1},{1,0},{2,3},{3,2},{4,5},{5,4},{6,7},{7,6},{8,9},{9,8},{10,11... | collective-permute-start | bytes 3145736 | tf_op jit(solution)/shard_map/ppermute | solution.py:26
  414.7 5.4 collective-permute-start.12
  418.5 49.4 %collective-permute-start.17 = (f32[4,16,16,256]{3,2,1,0:T(8,128)}, f32[4,16,16,256]{3,2,1,0:T(8,128)}, u32[]{:S(2)}, u32[]{:S(2)}) collective-permute-start(f32[4,16,16,256]{3,2,1,0:T(8,128)} %add.1263), channel_id=1, source_target_pairs={{0,2},{1,3},{2,0},{3,1},{4,6},{5,7},{6,4},{7,5},{8,10},{9,11},{10,... | collective-permute-start | bytes 3145736 | tf_op jit(solution)/shard_map/ppermute | solution.py:26
  421.0 4.4 collective-permute-start.13
  469.7 53.3 %collective-permute-start.18 = (f32[4,16,16,256]{3,2,1,0:T(8,128)S(1)}, f32[4,16,16,256]{3,2,1,0:T(8,128)}, u32[]{:S(2)}, u32[]{:S(2)}) collective-permute-start(f32[4,16,16,256]{3,2,1,0:T(8,128)S(1)} %add.1264), channel_id=1, source_target_pairs={{0,4},{1,5},{2,6},{3,7},{4,0},{5,1},{6,2},{7,3},{8,12},{9,13},{10,... | collective-permute-start | bytes 3145736 | tf_op jit(solution)/shard_map/ppermute | solution.py:26
  480.3 51.7 %all-to-all-start.3 = ((f32[32,1,4096]{2,1,0:T(1,128)}), f32[32,1,4096]{2,1,0:T(1,128)}, u32[]{:S(2)}, u32[]{:S(2)}) async-start(f32[32,1,4096]{2,1,0:T(1,128)} %reshape.92), calls=%async_computation.3 | async-start | bytes 1048576 | tf_op jit(solution)/shard_map/all_to_all | solution.py:178
  525.5 114.7 %collective-permute-start.19 = (f32[4,16,16,256]{3,2,1,0:T(8,128)}, f32[4,16,16,256]{3,2,1,0:T(8,128)}, u32[]{:S(2)}, u32[]{:S(2)}) collective-permute-start(f32[4,16,16,256]{3,2,1,0:T(8,128)} %add.1265), channel_id=1, source_target_pairs={{0,8},{1,9},{2,10},{3,11},{4,12},{5,13},{6,14},{7,15},{8,0},{9,1},... | collective-permute-start | bytes 3145736 | tf_op jit(solution)/shard_map/ppermute | solution.py:26
  545.5 4.4 collective-permute-start.14
  553.0 94.4 %collective-permute-start.15 = (f32[16,32,3,128]{3,1,2,0:T(8,128)}, f32[16,32,3,128]{3,1,2,0:T(8,128)}, u32[]{:S(2)}, u32[]{:S(2)}) collective-permute-start(f32[16,32,3,128]{3,1,2,0:T(8,128)} %slice.127), channel_id=1, source_target_pairs={{0,1},{1,2},{2,3},{3,4},{4,5},{5,6},{6,7},{7,8},{8,9},{9,10},{10,1... | collective-permute-start | bytes 2359304 | tf_op jit(solution)/shard_map/ppermute | solution.py:34
  641.9 26.5 %collective-permute-start.20 = (f32[4,16,16,256]{3,2,1,0:T(8,128)S(1)}, f32[4,16,16,256]{3,2,1,0:T(8,128)S(1)}, u32[]{:S(2)}, u32[]{:S(2)}) collective-permute-start(f32[4,16,16,256]{3,2,1,0:T(8,128)S(1)} %add.1266), channel_id=1, source_target_pairs={{0,16},{1,17},{2,18},{3,19},{4,20},{5,21},{6,22},{7,23},{8,24},{9,... | collective-permute-start | bytes 3145736 | tf_op jit(solution)/shard_map/ppermute | solution.py:26
  (26 other events, 500.1 us)
